TPU v7x, 128 devices: a whole 4x4x4 slice. The times are simulated.
128 devices in a mesh: ax: 8 (over y, z_lo), az: 16 (over z_hi, x, core).
Axes of the slice: x: 4, y: 4, z: 4 (z_hi: 2, z_lo: 2; z = z_hi * 2 + z_lo), core: 2. Of those that a mesh axis runs over, the one named last changes fastest.
Arguments:
- saved_flow: float32 [3, 256, 64, 1024], P(None, 'az', None, 'ax'), may hold values from -6 to 6
- saved_adjoint: float32 [3, 256, 64, 1024], P(None, 'az', None, 'ax'), may hold values from -6 to 6
- tangent: float32 [3, 256, 64, 1024], P(None, 'az', None, 'ax'), may hold values from -6 to 6
- second_adjoint: float32 [3, 256, 64, 1024], P(None, 'az', None, 'ax'), may hold values from -6 to 6
- radial_rate: float32 [64], replicated, may hold values from 1 to 100
Outputs:
- tangent_next: float32 [3, 256, 64, 1024], P(None, 'az', None, 'ax')
- second_next: float32 [3, 256, 64, 1024], P(None, 'az', None, 'ax')
All inputs are finite; a program needn't handle non-finite values.
Results may differ from a plain program's by a relative error of at most 0.00005.
Values sent between devices are 32-bit elements; how exact they have to be, the bound alone decides.
No kernel may reach another device: no remote copies, remote signals or barrier semaphores. Data moves between devices by JAX's collectives and lax.ppermute only.
A program may use at most 128 MiB of HBM per device.

v0:
```python
import math
import jax
import jax.numpy as jnp
from jax import lax
from jax.sharding import PartitionSpec as P

time_step = 0.1
viscosity = 0.005
axial_unit = 2.0 * math.pi / 20.0


def radial_table(count):
    points = jnp.arange(count, dtype=jnp.int32)[:, None]
    orders = jnp.arange(count, dtype=jnp.int32)[None, :]
    phases = orders * (2 * points + 1) % (4 * count)
    values = jnp.cos(phases.astype(jnp.float32) * (math.pi / (2.0 * count)))
    scales = jnp.where(orders == 0, math.sqrt(1.0 / count), math.sqrt(2.0 / count))
    return values * scales


def hartley_table(length):
    row_index = jnp.arange(length, dtype=jnp.int32)[:, None]
    col_index = jnp.arange(length, dtype=jnp.int32)[None, :]
    phases = row_index * col_index % length
    angles = phases.astype(jnp.float32) * (2.0 * math.pi / length)
    return (jnp.cos(angles) + jnp.sin(angles)) / math.sqrt(length)


def body(saved_flow, saved_adjoint, tangent, second_adjoint, radial_rate):
    components = tangent.shape[0]
    local_azimuth = tangent.shape[1]
    radial_count = tangent.shape[2]
    local_axial = tangent.shape[3]
    azimuth_count = local_azimuth * lax.axis_size("az")
    axial_count = local_axial * lax.axis_size("ax")
    radial = radial_table(radial_count)
    azimuth_table = hartley_table(azimuth_count)
    axial_table = hartley_table(axial_count)

    def along_azimuth(field):
        return jnp.einsum("nm,cmjk->cnjk", azimuth_table, field, precision=lax.Precision.HIGHEST)

    def along_axial(field):
        return jnp.einsum("nk,cmjk->cmjn", axial_table, field, precision=lax.Precision.HIGHEST)

    stacked = jnp.concatenate((saved_flow, saved_adjoint, tangent, second_adjoint), axis=0)
    grid = jnp.einsum("jr,cmrk->cmjk", radial, stacked, precision=lax.Precision.HIGHEST)
    halfway = along_azimuth(lax.all_to_all(grid, "az", split_axis=2, concat_axis=1, tiled=True))
    physical = along_axial(lax.all_to_all(halfway, "ax", split_axis=1, concat_axis=3, tiled=True))
    flow = physical[0:components]
    adjoint = physical[components : 2 * components]
    tang = physical[2 * components : 3 * components]
    second = physical[3 * components : 4 * components]
    flow_sum = jnp.sum(flow, axis=0)[None]
    adjoint_sum = jnp.sum(adjoint, axis=0)[None]
    tang_sum = jnp.sum(tang, axis=0)[None]
    second_sum = jnp.sum(second, axis=0)[None]
    tangent_rhs = flow * tang_sum + tang * flow_sum
    second_rhs = flow * second_sum + second * flow_sum + adjoint * tang_sum + tang * adjoint_sum
    products = jnp.concatenate((tangent_rhs, second_rhs), axis=0)
    partial_field = along_axial(products)
    turned = along_azimuth(
        lax.all_to_all(partial_field, "ax", split_axis=3, concat_axis=1, tiled=True)
    )
    spectral = jnp.einsum(
        "jr,cmjk->cmrk",
        radial,
        lax.all_to_all(turned, "az", split_axis=1, concat_axis=2, tiled=True),
        precision=lax.Precision.HIGHEST,
    )
    azimuth = lax.axis_index("az") * local_azimuth + jnp.arange(local_azimuth, dtype=jnp.int32)
    wave_azimuth = jnp.minimum(azimuth, azimuth_count - azimuth).astype(jnp.float32)
    axial = lax.axis_index("ax") * local_axial + jnp.arange(local_axial, dtype=jnp.int32)
    wave_axial = jnp.minimum(axial, axial_count - axial).astype(jnp.float32) * axial_unit
    total = (
        radial_rate[None, :, None]
        + (wave_azimuth**2)[:, None, None]
        + (wave_axial**2)[None, None, :]
    )
    denom = (1.0 + viscosity * total)[None]
    tangent_next = (tangent + time_step * spectral[0:components]) / denom
    second_next = (second_adjoint + time_step * spectral[components : 2 * components]) / denom
    return (tangent_next, second_next)


def solution(mesh):
    in_specs = (
        P(None, "az", None, "ax"),
        P(None, "az", None, "ax"),
        P(None, "az", None, "ax"),
        P(None, "az", None, "ax"),
        P(),
    )
    out_specs = (P(None, "az", None, "ax"), P(None, "az", None, "ax"))
    return jax.shard_map(body, mesh=mesh, in_specs=in_specs, out_specs=out_specs, check_vma=False)
```

profile of v0, /device:TPU:3, one launch (start us, length us, event | category | flops | bytes accessed | tf_op | source)
XLA Modules:
  0.0 556.9 jit_solution(827337466593299157)
XLA Ops:
  0.7 8.1 %fusion.23 = f32[12,16,64,128]{3,2,1,0:T(8,128)S(1)} fusion(f32[3,16,64,128]{3,2,1,0:T(8,128)} %param.8, f32[3,16,64,128]{3,2,1,0:T(8,128)} %param.7, f32[3,16,64,128]{3,2,1,0:T(8,128)} %param.6, f32[3,16,64,128]{3,2,1,0:T(8,128)} %param.5, f32[64]{0:T(128)S(1)} %compare_select_fusion, s32[64]{0:T(128)S(1)} %multiply_add_fusion.3), kind=kOutput, calls=%fused_computation.27 | convolution fusion | flops 1212739584 | bytes 12583424 | tf_op jit(solution)/shard_map/jr,cmrk->cmjk/dot_general | solution.py:47
  8.7 3.6 copy.33
  12.4 79.9 %all_to_all.72 = f32[12,16,64,128]{3,1,0,2:T(8,128)S(1)} all-to-all(f32[12,16,64,128]{3,1,0,2:T(8,128)S(1)} %copy.33), channel_id=1, replica_groups=mesh['ax'=8,'az'=16] {'az'}, dimensions={2} | all-to-all | bytes 12582912 | tf_op jit(solution)/shard_map/all_to_all | solution.py:48
  92.3 0.9 copy.35
  93.2 14.3 %convolution_bitcast_fusion = f32[12,256,4,128]{1,3,2,0:T(8,128)} fusion(f32[12,256,4,128]{3,1,2,0:T(8,128)S(1)} %bitcast.66), kind=kOutput, calls=%fused_computation.28 | convolution fusion | flops 4832886784 | bytes 12582912 | tf_op jit(solution)/shard_map/nm,cmjk->cnjk/dot_general | solution.py:41
  107.5 7.9 %copy.37 = f32[12,256,4,128]{3,2,0,1:T(4,128)} copy(f32[12,256,4,128]{1,3,2,0:T(8,128)} %convolution_bitcast_fusion) | data formatting | bytes 12582912 | tf_op jit(solution)/shard_map/nm,cmjk->cnjk/transpose | solution.py:41
  115.4 5.0 all-to-all-start.1
  120.4 17.7 %fusion.108 = f32[1024,1024,1,1]{1,0,3,2:T(8,128)} fusion(), kind=kLoop, calls=%fused_computation.19.clone.1 | loop fusion | flops 16777216 | bytes 4194304 | tf_op jit(solution)/shard_map/nk,cmjk->cmjn/dot_general | solution.py:44
  138.1 70.2 %all-to-all-done.1 = f32[12,256,4,128]{3,2,0,1:T(4,128)} async-done(((f32[12,256,4,128]{3,2,0,1:T(4,128)}), f32[12,256,4,128]{3,2,0,1:T(4,128)}, u32[]{:S(2)}, u32[]{:S(2)}) %all-to-all-start.1) | async-done | bytes 6291488 | tf_op jit(solution)/shard_map/all_to_all | solution.py:49
  208.3 5.0 copy.38
  213.2 144.5 %fusion = f32[12,32,4,1024]{3,1,2,0:T(8,128)S(1)} fusion(f32[12,4,8,4,8,128]{5,4,3,2,1,0:T(8,128)S(1)} %bitcast.70, f32[1024,1024,1,1]{1,0,3,2:T(8,128)S(1)} %copy-done.2), kind=kOutput, calls=%fused_computation | convolution fusion | flops 19327352832 | bytes 16777216 | tf_op jit(solution)/shard_map/nk,cmjk->cmjn/dot_general | solution.py:44
  357.8 0.8 slice_reduce_fusion.2
  358.6 1.3 multiply_add_fusion.1
  360.0 0.2 fusion.110
  360.2 29.0 %fusion.14 = f32[6,32,4,1024]{3,1,2,0:T(8,128)S(1)} fusion(f32[6,32,4,1024]{3,1,2,0:T(8,128)S(1)} %fusion.110), kind=kOutput, calls=%fused_computation.17 | convolution fusion | flops 9680453632 | bytes 6291456 | tf_op jit(solution)/shard_map/nk,cmjk->cmjn/dot_general | solution.py:44
  389.2 9.1 %copy.40 = f32[6,32,4,1024]{1,2,0,3:T(4,128)} copy(f32[6,32,4,1024]{3,1,2,0:T(8,128)S(1)} %fusion.14) | data formatting | bytes 6291456 | tf_op jit(solution)/shard_map/nk,cmjk->cmjn/dot_general | solution.py:44
  398.3 12.3 %reshape.77 = f32[8,1,98304]{2,1,0:T(1,128)} reshape(f32[1024,6,4,32]{3,2,1,0:T(4,128)} %bitcast.63) | data formatting | bytes 6291456
  410.6 41.0 %all_to_all.73 = f32[8,1,98304]{2,1,0:T(1,128)S(1)} all-to-all(f32[8,1,98304]{2,1,0:T(1,128)} %reshape.77), channel_id=1, replica_groups=mesh['ax'=8,'az'=16] {'ax'}, dimensions={0} | all-to-all | bytes 6291456 | tf_op jit(solution)/shard_map/all_to_all | solution.py:63
  451.6 0.5 broadcast.149
  452.1 11.1 %reduce = f32[8,98304]{1,0:T(8,128)} reduce(f32[8,1,98304]{2,1,0:T(1,128)S(1)} %all_to_all.73, f32[]{:T(128)} %broadcast.149), dimensions={1}, to_apply=%all_to_all.60.reduce_sub_computation | reduce | bytes 6291460 | tf_op jit(solution)/shard_map/all_to_all | solution.py:63
  463.2 13.3 %reshape.78 = f32[1024,6,4,32]{3,2,1,0:T(4,128)} reshape(f32[8,98304]{1,0:T(8,128)} %reduce) | data formatting | bytes 6291456
  476.5 11.4 %copy.56 = f32[6,32,4,8,128]{4,1,3,2,0:T(8,128)} copy(f32[6,32,4,8,128]{1,2,0,4,3:T(4,128)} %bitcast.64) | data formatting | bytes 6291456 | tf_op jit(solution)/shard_map/all_to_all | solution.py:63
  487.9 7.9 %convolution_bitcast_fusion.2 = f32[6,256,4,128]{1,3,2,0:T(8,128)S(1)} fusion(f32[6,256,4,128]{3,1,2,0:T(8,128)} %bitcast.69), kind=kOutput, calls=%fused_computation.30 | convolution fusion | flops 2416967680 | bytes 6291456 | tf_op jit(solution)/shard_map/nm,cmjk->cnjk/dot_general | solution.py:41
  495.8 3.0 copy.44
  498.8 6.7 %all-to-all-start.3 = ((f32[6,256,4,128]{3,2,0,1:T(4,128)}), f32[6,256,4,128]{3,2,0,1:T(4,128)S(1)}, u32[]{:S(2)}, u32[]{:S(2)}) async-start(f32[6,256,4,128]{3,2,0,1:T(4,128)} %copy.44), calls=%async_computation.3 | async-start | bytes 6291456 | tf_op jit(solution)/shard_map/all_to_all | solution.py:68
  505.5 0.1 broadcast_add_fusion
  505.6 1.0 multiply_add_fusion.2
  506.6 41.4 %all-to-all-done.3 = f32[6,256,4,128]{3,2,0,1:T(4,128)S(1)} async-done(((f32[6,256,4,128]{3,2,0,1:T(4,128)}), f32[6,256,4,128]{3,2,0,1:T(4,128)S(1)}, u32[]{:S(2)}, u32[]{:S(2)}) %all-to-all-start.3) | async-done | bytes 3145760 | tf_op jit(solution)/shard_map/all_to_all | solution.py:68
  548.0 0.6 copy.45
  548.6 2.0 copy.46
  550.7 3.3 convolution_bitcast_fusion.1
  554.0 2.5 fusion.27
  (14 shorter events, 0.1 us)
Async XLA Ops:
  115.4 92.9 %all-to-all-start.1 = ((f32[12,256,4,128]{3,2,0,1:T(4,128)}), f32[12,256,4,128]{3,2,0,1:T(4,128)}, u32[]{:S(2)}, u32[]{:S(2)}) async-start(f32[12,256,4,128]{3,2,0,1:T(4,128)} %copy.37), calls=%async_computation.1 | async-start | bytes 12582912 | tf_op jit(solution)/shard_map/all_to_all | solution.py:49
  208.3 5.0 copy-start.2
  498.8 6.7 %copy-start.4 = (f32[64]{0:T(128)S(1)}, f32[64]{0:T(128)}, u32[]{:S(2)}) copy-start(f32[64]{0:T(128)} %param.9) | copy-start | bytes 772
  498.8 49.2 %all-to-all-start.3 = ((f32[6,256,4,128]{3,2,0,1:T(4,128)}), f32[6,256,4,128]{3,2,0,1:T(4,128)S(1)}, u32[]{:S(2)}, u32[]{:S(2)}) async-start(f32[6,256,4,128]{3,2,0,1:T(4,128)} %copy.44), calls=%async_computation.3 | async-start | bytes 6291456 | tf_op jit(solution)/shard_map/all_to_all | solution.py:68
  550.6 3.3 copy-start
  550.6 3.3 copy-start.1
  550.7 3.3 copy-start.3
where the time goes:
time: 563 us; the launch traced here: 557 us
  matrix products  207 us (37%)
  blocking collectives  121 us (21%)
  waiting for transfers between devices  112 us (20%)
  local copies, waits for them, and re-layouts  69.6 us (12%)
  other arithmetic  34.8 us (6%)
  starting transfers between devices  11.7 us (2%)
    dot_general x2, matrix products, along_axial(): jnp.einsum('nk,cmjk->cmjn', axial_table, field, precision=lax.Precision.H...  174 us
    all_to_all x1, blocking collectives, body(): lax.all_to_all(grid, 'az', split_axis=2, concat_axis=1, tiled=True)  79.9 us
    all_to_all x1, waiting for transfers between devices, body(): lax.all_to_all(halfway, 'ax', split_axis=1, concat_axis=3, tiled=True)  70.2 us
    all_to_all x1, waiting for transfers between devices, body(): lax.all_to_all(turned, 'az', split_axis=1, concat_axis=2, tiled=True)  41.4 us
    all_to_all x1, blocking collectives, body(): lax.all_to_all(partial_field, 'ax', split_axis=3, concat_axis=1, tiled=True)  41 us
    unnamed x12, local copies, waits for them, and re-layouts  25.6 us
    dot_general x2, matrix products, along_azimuth(): jnp.einsum('nm,cmjk->cnjk', azimuth_table, field, precision=lax.Precision...  22.2 us
    dot_general x2, other arithmetic, along_axial(): jnp.einsum('nk,cmjk->cmjn', axial_table, field, precision=lax.Precision.H...  17.9 us
  transfers between devices with their start and end apart: 2, of which 2 were waited for; matrix products, arithmetic and copies ran while one was open for 3% of the time, Pallas kernels for 0%

commit v1 on v0

--- a/solution.py
+++ b/solution.py
@@ -7,6 +7,12 @@
 time_step = 0.1
 viscosity = 0.005
 axial_unit = 2.0 * math.pi / 20.0
+
+
+def swap_blocks(x, axis, split, join):
+    pieces = jnp.split(x, lax.axis_size(axis), axis=split)
+    got = lax.all_to_all(jnp.stack(pieces), axis, 0, 0)
+    return jnp.concatenate(got, axis=join)
 
 
 def radial_table(count):
@@ -59,9 +65,7 @@
     second_rhs = flow * second_sum + second * flow_sum + adjoint * tang_sum + tang * adjoint_sum
     products = jnp.concatenate((tangent_rhs, second_rhs), axis=0)
     partial_field = along_axial(products)
-    turned = along_azimuth(
-        lax.all_to_all(partial_field, "ax", split_axis=3, concat_axis=1, tiled=True)
-    )
+    turned = along_azimuth(swap_blocks(partial_field, "ax", 3, 1))
     spectral = jnp.einsum(
         "jr,cmjk->cmrk",
         radial,

time: 563 us -> 504 us (0.90)
  local copies, waits for them, and re-layouts: 69.6 us -> 23.9 us
  other arithmetic: 34.8 us -> 23.7 us
    unnamed x12 -> x17, local copies, waits for them, and re-layouts: 25.6 us -> 0.4 us
    all_to_all x2 -> x0, local copies, waits for them, and re-layouts: 11.9 us -> none  [body(): lax.all_to_all(partial_field, 'ax', split_axis=3, concat_axis=1, tiled=True)]
    all_to_all x1 -> x0, other arithmetic: 11.1 us -> none  [body(): lax.all_to_all(partial_field, 'ax', split_axis=3, concat_axis=1, tiled=True)]
    dot_general x1 -> x0, local copies, waits for them, and re-layouts: 9.06 us -> none  [along_axial(): jnp.einsum('nk,cmjk->cmjn', axial_table, field, precision=lax.Precision.H...]
  transfers between devices with their start and end apart: 2 -> 2, of which waited for: 2 -> 2; matrix products, arithmetic and copies ran while one was open for 3% -> 4% of each run, Pallas kernels for 0% -> 0%
where the time goes in v1:
time: 504 us; the launch traced here: 498 us
  matrix products  206 us (41%)
  blocking collectives  121 us (24%)
  waiting for transfers between devices  112 us (22%)
  local copies, waits for them, and re-layouts  23.9 us (5%)
  other arithmetic  23.7 us (5%)
  starting transfers between devices  11.7 us (2%)
    dot_general x2, matrix products, along_axial(): jnp.einsum('nk,cmjk->cmjn', axial_table, field, precision=lax.Precision.H...  174 us
    all_to_all x1, blocking collectives, body(): lax.all_to_all(grid, 'az', split_axis=2, concat_axis=1, tiled=True)  79.9 us
    all_to_all x1, waiting for transfers between devices, body(): lax.all_to_all(halfway, 'ax', split_axis=1, concat_axis=3, tiled=True)  70.1 us
    all_to_all x1, waiting for transfers between devices, body(): lax.all_to_all(turned, 'az', split_axis=1, concat_axis=2, tiled=True)  41.4 us
    all_to_all x1, blocking collectives, swap_blocks(): got = lax.all_to_all(jnp.stack(pieces), axis, 0, 0)  41 us
    dot_general x2, matrix products, along_azimuth(): jnp.einsum('nm,cmjk->cnjk', azimuth_table, field, precision=lax.Precision...  20.6 us
    dot_general x2, other arithmetic, along_axial(): jnp.einsum('nk,cmjk->cmjn', axial_table, field, precision=lax.Precision.H...  17.9 us
    transpose x2, local copies, waits for them, and re-layouts, along_azimuth(): jnp.einsum('nm,cmjk->cnjk', azimuth_table, field, precision=lax.Precision...  10.9 us
  transfers between devices with their start and end apart: 2, of which 2 were waited for; matrix products, arithmetic and copies ran while one was open for 4% of the time, Pallas kernels for 0%

profile of v1, /device:TPU:3, one launch (start us, length us, event | category | flops | bytes accessed | tf_op | source)
XLA Modules:
  0.0 498.5 jit_solution(4703808990904978728)
XLA Ops:
  0.7 8.1 %fusion.23 = f32[12,16,64,128]{3,2,1,0:T(8,128)S(1)} fusion(f32[3,16,64,128]{3,2,1,0:T(8,128)} %param.8, f32[3,16,64,128]{3,2,1,0:T(8,128)} %param.7, f32[3,16,64,128]{3,2,1,0:T(8,128)} %param.6, f32[3,16,64,128]{3,2,1,0:T(8,128)} %param.5, f32[64]{0:T(128)S(1)} %compare_select_fusion, s32[64]{0:T(128)S(1)} %multiply_add_fusion.3), kind=kOutput, calls=%fused_computation.27 | convolution fusion | flops 1212739584 | bytes 12583424 | tf_op jit(solution)/shard_map/jr,cmrk->cmjk/dot_general | solution.py:53
  8.8 3.6 copy.32
  12.4 79.9 %all_to_all.59 = f32[12,16,64,128]{3,1,0,2:T(8,128)S(1)} all-to-all(f32[12,16,64,128]{3,1,0,2:T(8,128)S(1)} %copy.32), channel_id=1, replica_groups=mesh['ax'=8,'az'=16] {'az'}, dimensions={2} | all-to-all | bytes 12582912 | tf_op jit(solution)/shard_map/all_to_all | solution.py:54
  92.4 0.9 copy.34
  93.2 14.4 %convolution_bitcast_fusion = f32[12,256,4,128]{1,3,2,0:T(8,128)} fusion(f32[12,256,4,128]{3,1,2,0:T(8,128)S(1)} %bitcast.91), kind=kOutput, calls=%fused_computation.28 | convolution fusion | flops 4832886784 | bytes 12582912 | tf_op jit(solution)/shard_map/nm,cmjk->cnjk/dot_general | solution.py:47
  107.6 8.0 %copy.36 = f32[12,256,4,128]{3,2,0,1:T(4,128)} copy(f32[12,256,4,128]{1,3,2,0:T(8,128)} %convolution_bitcast_fusion) | data formatting | bytes 12582912 | tf_op jit(solution)/shard_map/nm,cmjk->cnjk/transpose | solution.py:47
  115.6 5.1 %all-to-all-start.1 = ((f32[12,256,4,128]{3,2,0,1:T(4,128)}), f32[12,256,4,128]{3,2,0,1:T(4,128)}, u32[]{:S(2)}, u32[]{:S(2)}) async-start(f32[12,256,4,128]{3,2,0,1:T(4,128)} %copy.36), calls=%async_computation.1 | async-start | bytes 12582912 | tf_op jit(solution)/shard_map/all_to_all | solution.py:55
  120.7 17.7 %fusion.116 = f32[1024,1024,1,1]{1,0,3,2:T(8,128)} fusion(), kind=kLoop, calls=%fused_computation.19.clone.1 | loop fusion | flops 16777216 | bytes 4194304 | tf_op jit(solution)/shard_map/nk,cmjk->cmjn/dot_general | solution.py:50
  138.4 70.1 %all-to-all-done.1 = f32[12,256,4,128]{3,2,0,1:T(4,128)} async-done(((f32[12,256,4,128]{3,2,0,1:T(4,128)}), f32[12,256,4,128]{3,2,0,1:T(4,128)}, u32[]{:S(2)}, u32[]{:S(2)}) %all-to-all-start.1) | async-done | bytes 6291488 | tf_op jit(solution)/shard_map/all_to_all | solution.py:55
  208.5 5.0 copy.37
  213.5 144.5 %fusion = f32[12,32,4,1024]{3,1,2,0:T(8,128)S(1)} fusion(f32[12,4,8,4,8,128]{5,4,3,2,1,0:T(8,128)S(1)} %bitcast.96, f32[1024,1024,1,1]{1,0,3,2:T(8,128)S(1)} %copy-done.2), kind=kOutput, calls=%fused_computation | convolution fusion | flops 19327352832 | bytes 16777216 | tf_op jit(solution)/shard_map/nk,cmjk->cmjn/dot_general | solution.py:50
  358.0 0.8 slice_reduce_fusion.2
  358.8 1.3 multiply_add_fusion.1
  360.2 0.2 fusion.118
  360.4 29.1 %fusion.14 = f32[6,32,4,1024]{3,1,2,0:T(8,128)S(1)} fusion(f32[6,32,4,1024]{3,1,2,0:T(8,128)S(1)} %fusion.118), kind=kOutput, calls=%fused_computation.17 | convolution fusion | flops 9680453632 | bytes 6291456 | tf_op jit(solution)/shard_map/nk,cmjk->cmjn/dot_general | solution.py:50
  389.5 0.1 fusion.37
  389.6 0.1 fusion.36
  389.7 0.1 fusion.35
  389.9 0.1 fusion.31
  390.0 0.1 fusion.30
  390.0 41.0 %all_to_all.60 = f32[8,6,32,4,128]{4,2,3,1,0:T(8,128)S(1)} all-to-all(f32[8,6,32,4,128]{4,2,3,1,0:T(8,128)S(1)} %fusion.30), channel_id=1, replica_groups=mesh['ax'=8,'az'=16] {'ax'}, dimensions={0} | all-to-all | bytes 6291456 | tf_op jit(solution)/shard_map/all_to_all | solution.py:14
  431.0 0.4 copy.39
  431.5 6.3 %convolution_bitcast_fusion.2 = f32[6,256,4,128]{1,3,2,0:T(8,128)S(1)} fusion(f32[6,256,4,128]{3,1,2,0:T(8,128)S(1)} %bitcast.93), kind=kOutput, calls=%fused_computation.30 | convolution fusion | flops 2416967680 | bytes 6291456 | tf_op jit(solution)/shard_map/nm,cmjk->cnjk/dot_general | solution.py:47
  437.8 2.9 copy.41
  440.7 6.7 %all-to-all-start.3 = ((f32[6,256,4,128]{3,2,0,1:T(4,128)}), f32[6,256,4,128]{3,2,0,1:T(4,128)S(1)}, u32[]{:S(2)}, u32[]{:S(2)}) async-start(f32[6,256,4,128]{3,2,0,1:T(4,128)} %copy.41), calls=%async_computation.3 | async-start | bytes 6291456 | tf_op jit(solution)/shard_map/all_to_all | solution.py:72
  447.4 0.1 broadcast_add_fusion
  447.4 1.0 multiply_add_fusion.2
  448.4 41.4 %all-to-all-done.3 = f32[6,256,4,128]{3,2,0,1:T(4,128)S(1)} async-done(((f32[6,256,4,128]{3,2,0,1:T(4,128)}), f32[6,256,4,128]{3,2,0,1:T(4,128)S(1)}, u32[]{:S(2)}, u32[]{:S(2)}) %all-to-all-start.3) | async-done | bytes 3145760 | tf_op jit(solution)/shard_map/all_to_all | solution.py:72
  489.8 0.6 copy.42
  490.4 2.0 copy.43
  492.5 3.3 convolution_bitcast_fusion.1
  495.8 2.5 fusion.27
  (17 shorter events, 0.2 us)
Async XLA Ops:
  115.6 92.9 %all-to-all-start.1 = ((f32[12,256,4,128]{3,2,0,1:T(4,128)}), f32[12,256,4,128]{3,2,0,1:T(4,128)}, u32[]{:S(2)}, u32[]{:S(2)}) async-start(f32[12,256,4,128]{3,2,0,1:T(4,128)} %copy.36), calls=%async_computation.1 | async-start | bytes 12582912 | tf_op jit(solution)/shard_map/all_to_all | solution.py:55
  208.5 5.0 copy-start.2
  440.7 6.7 %copy-start.4 = (f32[64]{0:T(128)S(1)}, f32[64]{0:T(128)}, u32[]{:S(2)}) copy-start(f32[64]{0:T(128)} %param.9) | copy-start | bytes 772
  440.7 49.2 %all-to-all-start.3 = ((f32[6,256,4,128]{3,2,0,1:T(4,128)}), f32[6,256,4,128]{3,2,0,1:T(4,128)S(1)}, u32[]{:S(2)}, u32[]{:S(2)}) async-start(f32[6,256,4,128]{3,2,0,1:T(4,128)} %copy.41), calls=%async_computation.3 | async-start | bytes 6291456 | tf_op jit(solution)/shard_map/all_to_all | solution.py:72
  492.5 3.3 copy-start
  492.5 3.3 copy-start.1
  492.5 3.3 copy-start.3
